TPU v7x, 32 devices: a whole 2x2x4 slice. The times are simulated.
32 devices in a mesh: row: 4 (over z), col: 8 (over y, x, core).
Axes of the slice: x: 2, y: 2, z: 4, core: 2. Of those that a mesh axis runs over, the one named last changes fastest.
Arguments:
- kernel: bfloat16 [16384, 16384], P('row', 'col'), may hold values from -6 to 6
- labels: int32 [3, 16384], replicated, may hold values from 0 to 63, as said below
Outputs:
- distance: float32 [3, 16384, 64], P(None, ('row', 'col'))
- objective: float32 [3], replicated
Inputs may be any that keep to these rules, and one draw needn't show every extreme that they name: `labels`: in every iteration every cluster of 0 to 63 is named by at least one series.
All inputs are finite; a program needn't handle non-finite values.
Results may differ from a plain program's by a relative error of at most 0.0003.
Values sent between devices are 32-bit elements; how exact they have to be, the bound alone decides.
A program may use at most 64 MiB of HBM per device.

v0:
```python
import jax
import jax.numpy as jnp
from jax import lax
from jax.sharding import PartitionSpec as P

SERIES = 16384
CLUSTERS = 64
ITERS = 3


def shards(kernel, labels):
    rows_block, cols_block = kernel.shape
    slice_rows = rows_block // lax.axis_size("col")
    row_base = lax.axis_index("row") * rows_block
    col_base = lax.axis_index("col") * cols_block
    my_offset = lax.axis_index("col") * slice_rows
    clusters = jnp.arange(CLUSTERS, dtype=jnp.int32)
    col_labels = lax.dynamic_slice_in_dim(labels, col_base, cols_block, 1)
    block_labels = lax.dynamic_slice_in_dim(labels, row_base, rows_block, 1)
    counts = jnp.sum((labels[:, :, None] == clusters).astype(jnp.float32), axis=1)

    def encode(chosen):
        flat = chosen.T[:, :, None] == clusters[None, None, :]
        return flat.reshape(chosen.shape[1], -1).astype(jnp.bfloat16)

    local = jnp.dot(kernel, encode(col_labels), preferred_element_type=jnp.float32)
    whole = lax.psum(local, "col")
    totals = lax.psum(jnp.sum(encode(block_labels).astype(jnp.float32) * whole, axis=0), "row")
    sums = lax.dynamic_slice_in_dim(whole, my_offset, slice_rows, 0)
    sums, totals = (sums, totals)
    sums = sums.reshape(slice_rows, ITERS, CLUSTERS).transpose(1, 0, 2)
    totals = totals.reshape(ITERS, CLUSTERS)
    distance = -2.0 * sums / counts[:, None, :] + totals[:, None, :] / (counts * counts)[:, None, :]
    objective = 1.0 - jnp.sum(totals / counts, axis=1) / SERIES
    return (distance, objective)


def solution(mesh):
    return jax.shard_map(
        shards,
        mesh=mesh,
        in_specs=(P("row", "col"), P()),
        out_specs=(P(None, ("row", "col"), None), P()),
        check_vma=False,
    )
```

profile of v0, /device:TPU:0, one launch (start us, length us, event | category | flops | bytes accessed | tf_op | source)
XLA Modules:
  0.0 117.1 jit_solution(2459755366757021118)
XLA Ops:
  7.2 0.0 all-reduce.2.cloned.1.call-start
  7.2 0.1 eq.56
  7.3 0.8 dynamic-slice_bitcast_fusion.1
  8.1 0.3 bitcast_compare_fusion.1
  8.4 13.0 %convolution_bitcast_fusion = f32[4096,192]{0,1:T(8,128)} fusion(pred[2048,192]{0,1:T(32,128)(4,1)S(1)} %bitcast_compare_fusion.1, bf16[4096,2048]{1,0:T(8,128)(2,1)} %param.2), kind=kOutput, calls=%fused_computation.2 | convolution fusion | flops 3221225472 | bytes 20316160 | tf_op jit(solution)/shard_map/dot_general | solution.py:26
  21.4 0.0 copy-start
  21.4 0.0 all-reduce.2.cloned.1.call-update
  21.4 0.9 copy-done
  22.4 0.5 bitcast_compare_fusion
  22.9 2.0 %convert_reduce_fusion = f32[3,64]{1,0:T(4,128)S(1)} fusion(s32[3,16384]{1,0:T(4,128)S(1)} %copy-done), kind=kLoop, calls=%fused_computation | loop fusion | flops 9436992 | bytes 197376 | tf_op jit(solution)/shard_map/reduce_sum | solution.py:20
  24.9 68.7 %all-reduce.2.cloned.1.call-done = f32[4096,192]{0,1:T(8,128)} async-done(((f32[4096,192]{0,1:T(8,128)}), f32[4096,192]{0,1:T(8,128)}) %all-reduce.2.cloned.1.call-update) | async-done | bytes 3145744 | tf_op jit(solution)/shard_map/psum | solution.py:27
  93.6 2.4 %multiply_reduce_fusion = f32[192]{0:T(256)S(1)} fusion(f32[4096,192]{0,1:T(8,128)} %all-reduce.2.cloned.1.call-done, pred[4096,192]{0,1:T(8,128)(4,1)S(1)} %bitcast_compare_fusion), kind=kLoop, calls=%fused_computation.4 | loop fusion | flops 3145536 | bytes 3932928 | tf_op jit(solution)/shard_map/reduce_sum | solution.py:28
  96.0 0.1 broadcast_in_dim_reshape.3
  96.1 11.7 %psum.15 = f32[3,64]{1,0:T(4,128)S(1)} all-reduce(f32[3,64]{1,0:T(4,128)S(1)} %broadcast_in_dim_reshape.3), channel_id=1, replica_groups=mesh['row'=4,'col'=8] {'row'}, use_global_device_ids=true, to_apply=%region_3.0 | all-reduce | flops 192 | bytes 1536 | tf_op jit(solution)/shard_map/psum | solution.py:28
  107.8 0.1 divide_reduce_fusion
  107.9 0.5 multiply_subtract_fusion
  108.4 1.0 dynamic-slice_multiply_fusion
  109.4 0.9 add_bitcast_fusion
  (2 shorter events, 0.0 us)
Async XLA Ops:
  7.2 86.4 %all-reduce.2.cloned.1.call-start = ((), (), s32[]{:S(2)}) async-start(), calls=%async_computation | async-start | bytes 6291456 | tf_op jit(solution)/shard_map/psum | solution.py:27
  21.4 0.9 copy-start
Sparse Core Ops, SparseCore 0:
  21.6 71.9 all-reduce.1
where the time goes:
time: 117 us
  waiting for transfers between devices  68.8 us (59%)
  between operations  14.1 us (12%)
  matrix products  13 us (11%)
  blocking collectives  11.7 us (10%)
  other arithmetic  7.7 us (7%)
  local copies, waits for them, and re-layouts  1.86 us (2%)
    psum x1, waiting for transfers between devices, shards(): whole = lax.psum(local, 'col')  68.7 us
    dot_general x1, matrix products, shards(): jnp.dot(kernel, encode(col_labels), preferred_element_type=jnp.float32)  13 us
    psum x1, blocking collectives, shards(): lax.psum(jnp.sum(encode(block_labels).astype(jnp.float32) * whole, axis=0...  11.7 us
    reduce_sum x1, other arithmetic, shards(): jnp.sum(encode(block_labels).astype(jnp.float32) * whole, axis=0)  2.41 us
  transfers between devices with their start and end apart: 1, of which 1 were waited for; matrix products, arithmetic and copies ran while one was open for 2% of the time, Pallas kernels for 0%

commit v1 on v0

--- a/solution.py
+++ b/solution.py
@@ -2,6 +2,7 @@
 import jax.numpy as jnp
 from jax import lax
 from jax.sharding import PartitionSpec as P
+from jax.lax import all_gather
 
 SERIES = 16384
 CLUSTERS = 64
@@ -24,7 +25,7 @@
         return flat.reshape(chosen.shape[1], -1).astype(jnp.bfloat16)
 
     local = jnp.dot(kernel, encode(col_labels), preferred_element_type=jnp.float32)
-    whole = lax.psum(local, "col")
+    whole = jnp.sum(all_gather(local, "col"), 0)
     totals = lax.psum(jnp.sum(encode(block_labels).astype(jnp.float32) * whole, axis=0), "row")
     sums = lax.dynamic_slice_in_dim(whole, my_offset, slice_rows, 0)
     sums, totals = (sums, totals)

time: 117 us -> 201 us (1.72)
  waiting for transfers between devices: 68.8 us -> 124 us
  local copies, waits for them, and re-layouts: 1.86 us -> 24 us
  other arithmetic: 7.7 us -> 13.7 us
    all_gather x0 -> x1, waiting for transfers between devices: none -> 124 us  [shards(): whole = jnp.sum(all_gather(local, 'col'), 0)]
    psum x1 -> x0, waiting for transfers between devices: 68.7 us -> none  [shards(): whole = lax.psum(local, 'col')]
    unnamed x2 -> x5, local copies, waits for them, and re-layouts: 0.92 us -> 23 us
    reduce_sum x0 -> x1, other arithmetic: none -> 8.03 us  [shards(): whole = jnp.sum(all_gather(local, 'col'), 0)]
where the time goes in v1:
time: 201 us; the launch traced here: 200 us
  waiting for transfers between devices  124 us (62%)
  local copies, waits for them, and re-layouts  24 us (12%)
  between operations  14.1 us (7%)
  other arithmetic  13.7 us (7%)
  matrix products  13.1 us (7%)
  blocking collectives  11.7 us (6%)
    all_gather x1, waiting for transfers between devices, shards(): whole = jnp.sum(all_gather(local, 'col'), 0)  124 us
    unnamed x5, local copies, waits for them, and re-layouts  23 us
    dot_general x1, matrix products, shards(): jnp.dot(kernel, encode(col_labels), preferred_element_type=jnp.float32)  13.1 us
    psum x1, blocking collectives, shards(): lax.psum(jnp.sum(encode(block_labels).astype(jnp.float32) * whole, axis=0...  11.7 us
    reduce_sum x1, other arithmetic, shards(): whole = jnp.sum(all_gather(local, 'col'), 0)  8.03 us
  transfers between devices with their start and end apart: 1, of which 1 were waited for; matrix products, arithmetic and copies ran while one was open for 2% of the time, Pallas kernels for 0%

profile of v1, /device:TPU:0, one launch (start us, length us, event | category | flops | bytes accessed | tf_op | source)
XLA Modules:
  0.0 200.4 jit_solution(3998208494189982560)
XLA Ops:
  7.2 0.0 all-gather.3.cloned.1.call-start
  7.2 0.1 eq.60
  7.3 0.8 dynamic-slice_bitcast_fusion.1
  8.1 0.3 bitcast_compare_fusion.1
  8.4 13.1 %convolution_bitcast_fusion = f32[4096,192]{0,1:T(8,128)} fusion(pred[2048,192]{0,1:T(32,128)(4,1)S(1)} %bitcast_compare_fusion.1, bf16[4096,2048]{1,0:T(8,128)(2,1)} %param.2), kind=kOutput, calls=%fused_computation.3 | convolution fusion | flops 3221225472 | bytes 20316160 | tf_op jit(solution)/shard_map/dot_general | solution.py:27
  21.5 0.0 copy-start.1
  21.5 0.0 all-gather.3.cloned.1.call-update
  21.5 0.9 copy-done.1
  22.4 1.4 bitcast_compare_fusion
  23.8 2.0 convert_reduce_fusion
  25.8 123.8 %all-gather.3.cloned.1.call-done = f32[32768,192]{0,1:T(8,128)} async-done(((f32[4096,192]{0,1:T(8,128)}), f32[32768,192]{0,1:T(8,128)}) %all-gather.3.cloned.1.call-update) | async-done | bytes 25165840 | tf_op jit(solution)/shard_map/all_gather | solution.py:28
  149.6 22.1 %copy.5 = f32[24,8,8,4096]{3,2,1,0:T(8,128)S(1)} copy(f32[24,8,8,4096]{3,1,2,0:T(8,128)} %bitcast.20) | data formatting | bytes 50331648
  171.7 0.0 copy-start
  171.7 8.0 %bitcast_reduce_fusion = f32[4096,192]{0,1:T(8,128)S(1)} fusion(f32[24,8,8,4096]{3,2,1,0:T(8,128)S(1)} %copy.5), kind=kLoop, calls=%fused_computation | loop fusion | flops 5505024 | bytes 28311552 | tf_op jit(solution)/shard_map/reduce_sum | solution.py:28
  179.7 0.0 copy-done
  179.8 0.5 multiply_reduce_fusion
  180.3 0.1 broadcast_in_dim_reshape.3
  180.4 11.7 %psum.7 = f32[3,64]{1,0:T(4,128)S(1)} all-reduce(f32[3,64]{1,0:T(4,128)S(1)} %broadcast_in_dim_reshape.3), channel_id=1, replica_groups=mesh['row'=4,'col'=8] {'row'}, use_global_device_ids=true, to_apply=%region_3.0 | all-reduce | flops 192 | bytes 1536 | tf_op jit(solution)/shard_map/psum | solution.py:29
  192.1 0.1 divide_reduce_fusion
  192.2 0.5 multiply_subtract_fusion
  192.7 0.9 add_bitcast_fusion
  (3 shorter events, 0.0 us)
Async XLA Ops:
  7.2 142.4 %all-gather.3.cloned.1.call-start = ((), (), s32[]{:S(2)}) async-start(), calls=%async_computation | async-start | bytes 28311552 | tf_op jit(solution)/shard_map/all_gather | solution.py:28
  21.5 0.9 copy-start.1
  171.7 8.1 %copy-start = (pred[4096,192]{0,1:T(8,128)(4,1)S(1)}, pred[4096,192]{0,1:T(8,128)(4,1)}, u32[]{:S(2)}) copy-start(pred[4096,192]{0,1:T(8,128)(4,1)} %bitcast_compare_fusion) | copy-start | bytes 2359300
Sparse Core Ops, SparseCore 0:
  21.6 127.9 all-gather.2
